TPU v7x, 512 devices: a whole 4x4x16 slice. The times are simulated.
512 devices in a mesh: pipe: 8 (over y, core), ctx: 32 (over x, z_lo), tp: 2 (over z_hi).
Axes of the slice: x: 4, y: 4, z: 16 (z_hi: 2, z_lo: 8; z = z_hi * 8 + z_lo), core: 2. Of those that a mesh axis runs over, the one named last changes fastest.
Arguments:
- stream: bfloat16 [8, 4096, 4096], P('pipe', 'ctx', 'tp'), may hold values from -6 to 6
- queries: bfloat16 [8, 4096, 4096], P('pipe', 'ctx', 'tp'), may hold values from -5 to 5
- keys: bfloat16 [8, 4096, 1024], P('pipe', 'ctx', 'tp'), may hold values from -5 to 5
- values: bfloat16 [8, 4096, 1024], P('pipe', 'ctx', 'tp'), may hold values from -6 to 6
- segments: int32 [8, 4096], P('pipe', 'ctx'), may hold values from 0 to 5, never falling along the last dimension, each value on 1 to 2048 neighbouring positions
- norm_gain: bfloat16 [4096], P('tp'), may hold values from 0.25 to 1.75
Outputs:
- arrived: bfloat16 [8, 4096, 4096], P('pipe', 'ctx', 'tp')
- normed: bfloat16 [8, 4096, 4096], P('pipe', 'ctx', 'tp')
Inputs may be any that keep to these rules, and one draw needn't show every extreme that they name: `segments`: in each section's micro-batch the document number never falls along positions; each document holds 1 to half of 4096 positions, and one holds exactly half of 4096.
All inputs are finite; a program needn't handle non-finite values.
Results may differ from a plain program's by a relative error of at most 0.006.
Values may be sent and summed in bfloat16 or wider, within the bound.
A program may use at most 128 MiB of HBM per device.

v0:
```python
import jax
import jax.numpy as jnp
from jax import lax
from jax.sharding import PartitionSpec as P

QUERY_HEADS = 32
HEAD_SIZE = 128


def from_behind(block, axis, distance):
    devices = range(lax.axis_size(axis))
    route = [((i - distance) % len(devices), i) for i in devices]
    return lax.ppermute(block, axis, route)


def per_device(stream, queries, keys, values, segments, norm_gain):
    row_count = stream.shape[1]
    kv_width = keys.shape[2]
    kv_heads = kv_width // HEAD_SIZE
    query_group_size = queries.shape[2] // kv_width
    score_scale = HEAD_SIZE ** (-0.5)
    ctx_index = lax.axis_index("ctx")
    query_head_stack = (
        queries[0]
        .reshape(row_count, kv_heads, query_group_size, HEAD_SIZE)
        .transpose(1, 2, 0, 3)
        .reshape(kv_heads, query_group_size * row_count, HEAD_SIZE)
    )
    own_pos = ctx_index * row_count + jnp.arange(row_count, dtype=jnp.int32)
    query_pos = jnp.tile(own_pos, query_group_size)
    query_seg = jnp.tile(segments[0], query_group_size)
    query_row_block = query_group_size * row_count
    key_piece = lax.all_gather(keys[0], "ctx", axis=0, tiled=True)
    running_max = jnp.full((kv_heads, query_row_block), -1e30, jnp.float32)
    key_count = key_piece.shape[0]
    key_head_stack = key_piece.reshape(key_count, kv_heads, HEAD_SIZE)
    value_head_stack = lax.all_gather(values[0], "ctx", axis=0, tiled=True).reshape(
        key_count, kv_heads, HEAD_SIZE
    )
    scores = (
        jnp.einsum(
            "hrd,khd->hrk", query_head_stack, key_head_stack, preferred_element_type=jnp.float32
        )
        * score_scale
    )
    key_pos = jnp.arange(key_count, dtype=jnp.int32)
    allowed = (
        (key_pos[None, :] <= query_pos[:, None])
        & (lax.all_gather(segments[0], "ctx", axis=0, tiled=True)[None, :] == query_seg[:, None])
        & jnp.bool_(True)
    )
    scores = jnp.where(allowed[None], scores, -1e30)
    new_max = jnp.maximum(running_max, jnp.max(scores, axis=-1))
    weights = jnp.where(allowed[None], jnp.exp(scores - new_max[..., None]), 0.0)
    new_sum = jnp.sum(weights, axis=-1)
    new_acc = jnp.einsum(
        "hrk,khd->hrd",
        weights.astype(jnp.bfloat16),
        value_head_stack,
        preferred_element_type=jnp.float32,
    )
    final_state = (new_max, new_sum, new_acc)
    running_max, running_sum, running_acc = final_state
    mixed = (running_acc / running_sum[..., None]).astype(jnp.bfloat16)
    attended = (
        mixed.reshape(kv_heads, query_group_size, row_count, HEAD_SIZE)
        .transpose(2, 0, 1, 3)
        .reshape(row_count, kv_width * query_group_size)
    )
    attended = lax.optimization_barrier(attended).astype(jnp.float32)
    advanced = (stream[0].astype(jnp.float32) + attended).astype(jnp.bfloat16)
    arrived = from_behind(advanced[None], "pipe", 1)
    wide = arrived.astype(jnp.float32)
    squares = jnp.sum(wide * wide, axis=-1)
    totals = lax.psum(squares, "tp")
    inverse = lax.rsqrt(totals / (QUERY_HEADS * HEAD_SIZE) + 1e-05)
    normed = (wide * inverse[..., None] * norm_gain.astype(jnp.float32)).astype(jnp.bfloat16)
    return (arrived, normed)


def solution(mesh):
    in_specs = (
        P("pipe", "ctx", "tp"),
        P("pipe", "ctx", "tp"),
        P("pipe", "ctx", "tp"),
        P("pipe", "ctx", "tp"),
        P("pipe", "ctx"),
        P("tp"),
    )
    out_specs = (P("pipe", "ctx", "tp"), P("pipe", "ctx", "tp"))
    return jax.shard_map(
        per_device, mesh=mesh, in_specs=in_specs, out_specs=out_specs, check_vma=False
    )
```

profile of v0, /device:TPU:8, one launch (start us, length us, event | category | flops | bytes accessed | tf_op | source)
XLA Modules:
  0.0 487.5 jit_solution(13736906237650311648)
XLA Ops:
  7.2 0.0 all-gather.6.cloned.1.call-start
  7.2 1.7 copy.11
  8.9 0.0 all-gather.6.cloned.1.call-update
  8.9 0.0 all-gather.8.cloned.1.call-start
  8.9 1.7 copy.13
  10.6 0.0 all-gather.8.cloned.1.call-update
  10.6 1.4 reshape_squeeze.3
  12.0 0.1 copy.10
  12.2 125.1 %all-gather = s32[1,4096]{1,0:T(1,128)S(1)} all-gather(s32[1,128]{1,0:T(1,128)} %param.10), channel_id=2, replica_groups=mesh['pipe'=8,'ctx'=32,'tp'=2] {'ctx'}, dimensions={1}, use_global_device_ids=true | all-gather | bytes 16896 | tf_op jit(solution)/shard_map/all_gather | solution.py:49
  137.3 0.7 broadcast_bitcast_fusion
  138.0 2.2 fusion.6
  140.2 88.0 %all-gather.6.cloned.1.call-done = bf16[1,4096,512]{1,2,0:T(8,128)(2,1)} async-done(((bf16[1,128,512]{1,2,0:T(8,128)(2,1)}), bf16[1,4096,512]{1,2,0:T(8,128)(2,1)}) %all-gather.6.cloned.1.call-update) | async-done | bytes 4194320 | tf_op jit(solution)/shard_map/all_gather | solution.py:33
  228.2 16.7 %fusion = (f32[4,512]{1,0:T(4,128)S(1)}, f32[4,512,4096]{2,1,0:T(8,128)}) fusion(pred[512,4096]{1,0:T(8,128)(4,1)S(1)} %fusion.6, bf16[4,512,128]{2,1,0:T(8,128)(2,1)S(1)} %bitcast.25, bf16[4096,4,128]{0,2,1:T(8,128)(2,1)} %bitcast.24), kind=kOutput, calls=%fused_computation.2 | convolution fusion | flops 2172647424 | bytes 40378368 | tf_op jit(solution)/shard_map/hrd,khd->hrk/dot_general | solution.py:41
  244.9 15.6 %fusion.1 = f32[4,512]{1,0:T(4,128)S(1)} fusion(f32[4,512,4096]{2,1,0:T(8,128)} %get-tuple-element.3, f32[4,512]{1,0:T(4,128)S(1)} %broadcast_maximum_fusion, pred[512,4096]{1,0:T(8,128)(4,1)S(1)} %fusion.6), kind=kLoop, calls=%fused_computation.3 | loop fusion | flops 41940992 | bytes 35667968 | tf_op jit(solution)/shard_map/reduce_sum | solution.py:55
  260.5 178.8 %all-gather.8.cloned.1.call-done = bf16[1,4096,512]{1,2,0:T(8,128)(2,1)} async-done(((bf16[1,128,512]{1,2,0:T(8,128)(2,1)}), bf16[1,4096,512]{1,2,0:T(8,128)(2,1)}) %all-gather.8.cloned.1.call-update) | async-done | bytes 4194320 | tf_op jit(solution)/shard_map/all_gather | solution.py:37
  439.3 0.0 copy-start
  439.3 0.0 copy-start.1
  439.3 16.1 %divide_convert_fusion = bf16[4,512,128]{2,1,0:T(8,128)(2,1)S(1)} fusion(bf16[4096,4,128]{0,2,1:T(8,128)(2,1)} %bitcast.31, f32[4,512,4096]{2,1,0:T(8,128)} %get-tuple-element.3, f32[4,512]{1,0:T(4,128)S(1)} %broadcast_maximum_fusion, pred[512,4096]{1,0:T(8,128)(4,1)S(1)} %fusion.6, f32[4,512]{1,0:T(4,128)S(1)} %fusion.1), kind=kOutput, calls=%fused_computation.16 | convolution fusion | flops 2189950976 | bytes 40386560 | tf_op jit(solution)/shard_map/hrk,khd->hrd/dot_general | solution.py:56
  455.4 0.4 copy.15
  455.8 0.4 reshape.92
  456.2 0.0 copy-done
  456.2 0.1 fusion.13
  456.4 0.0 collective-permute-start
  456.4 0.0 copy-done.1
  456.4 8.6 %collective-permute-done = bf16[1,128,2048]{2,1,0:T(8,128)(2,1)S(1)} collective-permute-done((bf16[1,128,2048]{2,1,0:T(8,128)(2,1)S(1)}, bf16[1,128,2048]{2,1,0:T(8,128)(2,1)S(1)}, u32[]{:S(2)}, u32[]{:S(2)}) %collective-permute-start) | collective-permute-done | bytes 524320 | tf_op jit(solution)/shard_map/ppermute | solution.py:13
  465.0 0.2 fusion.7
  465.2 13.6 %psum.7 = f32[1,128]{1,0:T(1,128)S(1)} all-reduce(f32[1,128]{1,0:T(1,128)S(1)} %bitcast.30), channel_id=1, replica_groups=mesh['pipe'=8,'ctx'=32,'tp'=2] {'tp'}, use_global_device_ids=true, to_apply=%region_3.4 | all-reduce | flops 128 | bytes 1024 | tf_op jit(solution)/shard_map/psum | solution.py:75
  478.8 1.0 fusion.9
  479.8 0.8 copy.19
  (4 shorter events, 0.0 us)
Async XLA Ops:
  7.2 221.0 %all-gather.6.cloned.1.call-start = ((), (), s32[]{:S(2)}) async-start(), calls=%async_computation | async-start | bytes 4325376 | tf_op jit(solution)/shard_map/all_gather | solution.py:33
  8.9 430.4 %all-gather.8.cloned.1.call-start = ((), (), s32[]{:S(2)}) async-start(), calls=%async_computation.1 | async-start | bytes 4325376 | tf_op jit(solution)/shard_map/all_gather | solution.py:37
  439.3 17.0 %copy-start = (bf16[1,128,2048]{2,1,0:T(8,128)(2,1)S(1)}, bf16[1,128,2048]{2,1,0:T(8,128)(2,1)}, u32[]{:S(2)}) copy-start(bf16[1,128,2048]{2,1,0:T(8,128)(2,1)} %param.6) | copy-start | bytes 1572868
  439.3 17.1 %copy-start.1 = (bf16[2048]{0:T(1024)(128)(2,1)S(1)}, bf16[2048]{0:T(1024)(128)(2,1)}, u32[]{:S(2)}) copy-start(bf16[2048]{0:T(1024)(128)(2,1)} %param.11) | copy-start | bytes 12292
  456.4 8.6 %collective-permute-start = (bf16[1,128,2048]{2,1,0:T(8,128)(2,1)S(1)}, bf16[1,128,2048]{2,1,0:T(8,128)(2,1)S(1)}, u32[]{:S(2)}, u32[]{:S(2)}) collective-permute-start(bf16[1,128,2048]{2,1,0:T(8,128)(2,1)S(1)} %fusion.13), channel_id=1, source_target_pairs={{448,0},{0,64},{64,128},{128,192},{192,256},{256,320},{320,384},{3... | collective-permute-start | bytes 1572872 | tf_op jit(solution)/shard_map/ppermute | solution.py:13
Sparse Core Ops, SparseCore 0:
  10.6 217.5 all-gather.5
  230.8 208.4 all-gather.7
where the time goes:
time: 488 us; the launch traced here: 487 us
  waiting for transfers between devices  275 us (56%)
  blocking collectives  139 us (28%)
  matrix products  32.8 us (7%)
  other arithmetic  19.2 us (4%)
  between operations  14.1 us (3%)
  local copies, waits for them, and re-layouts  7.12 us (1%)
    all_gather x1, waiting for transfers between devices, per_device(): lax.all_gather(values[0], 'ctx', axis=0, tiled=True)  179 us
    all_gather x1, blocking collectives, per_device(): lax.all_gather(segments[0], 'ctx', axis=0, tiled=True)[None, :]  125 us
    all_gather x1, waiting for transfers between devices, per_device(): key_piece = lax.all_gather(keys[0], 'ctx', axis=0, tiled=True)  88 us
    dot_general x1, matrix products, per_device(): jnp.einsum('hrd,khd->hrk', query_head_stack, key_head_stack, preferred_el...  16.7 us
    dot_general x1, matrix products, per_device(): jnp.einsum('hrk,khd->hrd', weights.astype(jnp.bfloat16), value_head_stack...  16.1 us
    reduce_sum x1, other arithmetic, per_device(): new_sum = jnp.sum(weights, axis=-1)  15.6 us
    psum x1, blocking collectives, per_device(): totals = lax.psum(squares, 'tp')  13.6 us
  transfers between devices with their start and end apart: 3, of which 3 were waited for; matrix products, arithmetic and copies ran while one was open for 8% of the time, Pallas kernels for 0%

commit v1 on v0

--- a/solution.py
+++ b/solution.py
@@ -46,7 +46,12 @@
     key_pos = jnp.arange(key_count, dtype=jnp.int32)
     allowed = (
         (key_pos[None, :] <= query_pos[:, None])
-        & (lax.all_gather(segments[0], "ctx", axis=0, tiled=True)[None, :] == query_seg[:, None])
+        & (
+            jnp.concatenate(
+                lax.all_to_all(jnp.stack([segments[0]] * lax.axis_size("ctx")), "ctx", 0, 0), axis=0
+            )[None, :]
+            == query_seg[:, None]
+        )
         & jnp.bool_(True)
     )
     scores = jnp.where(allowed[None], scores, -1e30)

time: 488 us -> 487 us (level)
  blocking collectives: 139 us -> 13.6 us
  waiting for transfers between devices: 275 us -> 383 us
  starting transfers between devices: 0.1 us -> 15.5 us
    all_gather x1 -> x0, blocking collectives: 125 us -> none  [per_device(): lax.all_gather(segments[0], 'ctx', axis=0, tiled=True)[None, :]]
    all_gather x1, waiting for transfers between devices: 88 us -> 186 us  [per_device(): key_piece = lax.all_gather(keys[0], 'ctx', axis=0, tiled=True)]
    all_to_all x0 -> x1, starting transfers between devices: none -> 15.4 us  [per_device(): lax.all_to_all(jnp.stack([segments[0]] * lax.axis_size('ctx')), 'ctx', 0, 0)]
    all_to_all x0 -> x1, waiting for transfers between devices: none -> 10.3 us  [per_device(): lax.all_to_all(jnp.stack([segments[0]] * lax.axis_size('ctx')), 'ctx', 0, 0)]
  transfers between devices with their start and end apart: 3 -> 4, of which waited for: 3 -> 4; matrix products, arithmetic and copies ran while one was open for 8% -> 8% of each run, Pallas kernels for 0% -> 0%
where the time goes in v1:
time: 487 us
  waiting for transfers between devices  383 us (79%)
  matrix products  32.8 us (7%)
  other arithmetic  19.2 us (4%)
  starting transfers between devices  15.5 us (3%)
  between operations  14.1 us (3%)
  blocking collectives  13.6 us (3%)
  local copies, waits for them, and re-layouts  8.39 us (2%)
    all_gather x1, waiting for transfers between devices, per_device(): key_piece = lax.all_gather(keys[0], 'ctx', axis=0, tiled=True)  186 us
    all_gather x1, waiting for transfers between devices, per_device(): lax.all_gather(values[0], 'ctx', axis=0, tiled=True)  178 us
    dot_general x1, matrix products, per_device(): jnp.einsum('hrd,khd->hrk', query_head_stack, key_head_stack, preferred_el...  16.7 us
    dot_general x1, matrix products, per_device(): jnp.einsum('hrk,khd->hrd', weights.astype(jnp.bfloat16), value_head_stack...  16.1 us
    reduce_sum x1, other arithmetic, per_device(): new_sum = jnp.sum(weights, axis=-1)  15.6 us
    all_to_all x1, starting transfers between devices, per_device(): lax.all_to_all(jnp.stack([segments[0]] * lax.axis_size('ctx')), 'ctx', 0, 0)  15.4 us
    psum x1, blocking collectives, per_device(): totals = lax.psum(squares, 'tp')  13.6 us
    all_to_all x1, waiting for transfers between devices, per_device(): lax.all_to_all(jnp.stack([segments[0]] * lax.axis_size('ctx')), 'ctx', 0, 0)  10.3 us
  transfers between devices with their start and end apart: 4, of which 4 were waited for; matrix products, arithmetic and copies ran while one was open for 8% of the time, Pallas kernels for 0%

profile of v1, /device:TPU:8, one launch (start us, length us, event | category | flops | bytes accessed | tf_op | source)
XLA Modules:
  0.0 486.9 jit_solution(3049231343508701010)
XLA Ops:
  7.2 0.0 all-gather.5.cloned.1.call-start
  7.2 1.7 copy.11
  8.9 0.0 all-gather.5.cloned.1.call-update
  8.9 0.0 all-gather.7.cloned.1.call-start
  8.9 1.7 copy.13
  10.6 0.0 all-gather.7.cloned.1.call-update
  10.6 1.3 stack.3
  11.9 15.4 %all-to-all-start = ((s32[32,1,128]{2,1,0:T(1,128)}), s32[32,1,128]{2,1,0:T(1,128)S(1)}, u32[]{:S(2)}, u32[]{:S(2)}) async-start(s32[32,1,128]{2,1,0:T(1,128)} %stack.3), calls=%async_computation | async-start | bytes 32768 | tf_op jit(solution)/shard_map/all_to_all | solution.py:51
  27.3 0.7 broadcast_bitcast_fusion
  28.0 1.4 reshape_squeeze.3
  29.4 0.1 copy.10
  29.5 10.3 %all-to-all-done = s32[32,1,128]{2,1,0:T(1,128)S(1)} async-done(((s32[32,1,128]{2,1,0:T(1,128)}), s32[32,1,128]{2,1,0:T(1,128)S(1)}, u32[]{:S(2)}, u32[]{:S(2)}) %all-to-all-start) | async-done | bytes 16416 | tf_op jit(solution)/shard_map/all_to_all | solution.py:51
  39.8 2.2 fusion.6
  42.0 186.2 %all-gather.5.cloned.1.call-done = bf16[1,4096,512]{1,2,0:T(8,128)(2,1)} async-done(((bf16[1,128,512]{1,2,0:T(8,128)(2,1)}), bf16[1,4096,512]{1,2,0:T(8,128)(2,1)}) %all-gather.5.cloned.1.call-update) | async-done | bytes 4194320 | tf_op jit(solution)/shard_map/all_gather | solution.py:33
  228.2 16.7 %fusion = (f32[4,512]{1,0:T(4,128)S(1)}, f32[4,512,4096]{2,1,0:T(8,128)}) fusion(pred[512,4096]{1,0:T(8,128)(4,1)S(1)} %fusion.6, bf16[4,512,128]{2,1,0:T(8,128)(2,1)S(1)} %bitcast.25, bf16[4096,4,128]{0,2,1:T(8,128)(2,1)} %bitcast.24), kind=kOutput, calls=%fused_computation.2 | convolution fusion | flops 2172647424 | bytes 40378368 | tf_op jit(solution)/shard_map/hrd,khd->hrk/dot_general | solution.py:41
  244.9 15.6 %fusion.1 = f32[4,512]{1,0:T(4,128)S(1)} fusion(f32[4,512,4096]{2,1,0:T(8,128)} %get-tuple-element.3, f32[4,512]{1,0:T(4,128)S(1)} %broadcast_maximum_fusion, pred[512,4096]{1,0:T(8,128)(4,1)S(1)} %fusion.6), kind=kLoop, calls=%fused_computation.3 | loop fusion | flops 41940992 | bytes 35667968 | tf_op jit(solution)/shard_map/reduce_sum | solution.py:60
  260.5 178.2 %all-gather.7.cloned.1.call-done = bf16[1,4096,512]{1,2,0:T(8,128)(2,1)} async-done(((bf16[1,128,512]{1,2,0:T(8,128)(2,1)}), bf16[1,4096,512]{1,2,0:T(8,128)(2,1)}) %all-gather.7.cloned.1.call-update) | async-done | bytes 4194320 | tf_op jit(solution)/shard_map/all_gather | solution.py:37
  438.8 0.0 copy-start
  438.8 0.0 copy-start.1
  438.8 16.1 %divide_convert_fusion = bf16[4,512,128]{2,1,0:T(8,128)(2,1)S(1)} fusion(bf16[4096,4,128]{0,2,1:T(8,128)(2,1)} %bitcast.32, f32[4,512,4096]{2,1,0:T(8,128)} %get-tuple-element.3, f32[4,512]{1,0:T(4,128)S(1)} %broadcast_maximum_fusion, pred[512,4096]{1,0:T(8,128)(4,1)S(1)} %fusion.6, f32[4,512]{1,0:T(4,128)S(1)} %fusion.1), kind=kOutput, calls=%fused_computation.16 | convolution fusion | flops 2189950976 | bytes 40386560 | tf_op jit(solution)/shard_map/hrk,khd->hrd/dot_general | solution.py:61
  454.9 0.4 copy.15
  455.3 0.4 reshape.103
  455.7 0.0 copy-done
  455.7 0.1 fusion.13
  455.8 0.0 collective-permute-start
  455.9 0.0 copy-done.1
  455.9 8.6 %collective-permute-done = bf16[1,128,2048]{2,1,0:T(8,128)(2,1)S(1)} collective-permute-done((bf16[1,128,2048]{2,1,0:T(8,128)(2,1)S(1)}, bf16[1,128,2048]{2,1,0:T(8,128)(2,1)S(1)}, u32[]{:S(2)}, u32[]{:S(2)}) %collective-permute-start) | collective-permute-done | bytes 524320 | tf_op jit(solution)/shard_map/ppermute | solution.py:13
  464.5 0.2 fusion.7
  464.6 13.6 %psum.7 = f32[1,128]{1,0:T(1,128)S(1)} all-reduce(f32[1,128]{1,0:T(1,128)S(1)} %bitcast.31), channel_id=1, replica_groups=mesh['pipe'=8,'ctx'=32,'tp'=2] {'tp'}, use_global_device_ids=true, to_apply=%region_3.4 | all-reduce | flops 128 | bytes 1024 | tf_op jit(solution)/shard_map/psum | solution.py:80
  478.3 1.0 fusion.9
  479.3 0.8 copy.19
  (4 shorter events, 0.0 us)
Async XLA Ops:
  7.2 221.1 %all-gather.5.cloned.1.call-start = ((), (), s32[]{:S(2)}) async-start(), calls=%async_computation.1 | async-start | bytes 4325376 | tf_op jit(solution)/shard_map/all_gather | solution.py:33
  8.9 429.9 %all-gather.7.cloned.1.call-start = ((), (), s32[]{:S(2)}) async-start(), calls=%async_computation.2 | async-start | bytes 4325376 | tf_op jit(solution)/shard_map/all_gather | solution.py:37
  11.9 27.9 %all-to-all-start = ((s32[32,1,128]{2,1,0:T(1,128)}), s32[32,1,128]{2,1,0:T(1,128)S(1)}, u32[]{:S(2)}, u32[]{:S(2)}) async-start(s32[32,1,128]{2,1,0:T(1,128)} %stack.3), calls=%async_computation | async-start | bytes 32768 | tf_op jit(solution)/shard_map/all_to_all | solution.py:51
  438.8 16.9 %copy-start = (bf16[1,128,2048]{2,1,0:T(8,128)(2,1)S(1)}, bf16[1,128,2048]{2,1,0:T(8,128)(2,1)}, u32[]{:S(2)}) copy-start(bf16[1,128,2048]{2,1,0:T(8,128)(2,1)} %param.6) | copy-start | bytes 1572868
  438.8 17.1 %copy-start.1 = (bf16[2048]{0:T(1024)(128)(2,1)S(1)}, bf16[2048]{0:T(1024)(128)(2,1)}, u32[]{:S(2)}) copy-start(bf16[2048]{0:T(1024)(128)(2,1)} %param.11) | copy-start | bytes 12292
  455.8 8.6 %collective-permute-start = (bf16[1,128,2048]{2,1,0:T(8,128)(2,1)S(1)}, bf16[1,128,2048]{2,1,0:T(8,128)(2,1)S(1)}, u32[]{:S(2)}, u32[]{:S(2)}) collective-permute-start(bf16[1,128,2048]{2,1,0:T(8,128)(2,1)S(1)} %fusion.13), channel_id=1, source_target_pairs={{448,0},{0,64},{64,128},{128,192},{192,256},{256,320},{320,384},{3... | collective-permute-start | bytes 1572872 | tf_op jit(solution)/shard_map/ppermute | solution.py:13
Sparse Core Ops, SparseCore 0:
  10.6 217.6 all-gather.4
  230.8 207.8 all-gather.6
